TPU v7x, 32 devices: a whole 2x2x4 slice. The times are simulated.
32 devices in a mesh: pb: 2 (over x), pair: 16 (over z, y, core).
Axes of the slice: x: 2, y: 2, z: 4, core: 2. Of those that a mesh axis runs over, the one named last changes fastest.
Arguments:
- screened: bfloat16 [32, 2048, 256], P(('pb', 'pair')), parts along dimension 0, may hold values from -0.1875 to 0.1875
- conduction: bfloat16 [20480, 2048], P(('pb', 'pair')), parts along dimension 0, may hold values from -6 to 6
- valence: bfloat16 [512, 2048], P(('pb', 'pair')), parts along dimension 0, may hold values from -0.125 to 0.125
- owners: int32 [8], P('pb'), parts along dimension 0, may hold values from 0 to 15, as said below
- column_block: int32 [8], P('pb'), parts along dimension 0, may hold values from 0 to 7
Outputs:
- kernel: bfloat16 [512, 10240], P('pb', 'pair'), parts along dimension 0
There are 2 independent parts, one for each index of `pb`. A program takes and returns all parts, laid end to end along the dimension named above; each array names one. Nothing has to cross between parts.
Inputs may be any that keep to these rules, and one draw needn't show every extreme that they name: `owners`: the 4 entries are distinct devices of the group.
All inputs are finite; a program needn't handle non-finite values.
Results may differ from a plain program's by a relative error of at most 0.001.
Values may be sent and summed in bfloat16 or wider, within the bound.
A program may use at most 128 MiB of HBM per device.

v0:
```python
import functools

import jax
import jax.numpy as jnp
from jax import lax
from jax.experimental import pallas as pl
from jax.experimental.pallas import tpu as pltpu
from jax.sharding import PartitionSpec as P

MESH = pl.DeviceIdType.MESH
REACH = 3
PIECES = 1


def grid_of(n):
    chips = n // 2
    b = 1
    while b * b * 4 <= chips:
        b *= 2
    return chips // b, b


def events_of(A, B):
    events = []
    for d in range(A):
        start = 1.0 * (-(-d // REACH)) + 0.3 * ((d - 1) % REACH if d else 0)
        last = start + 0.95 * (B - 1)
        for da in (1, -1) if d else (0,):
            for h in range(PIECES):
                when = start + 0.3 * h / PIECES
                events.append((when, 0, h, "a", d, da, 0, 0))
                for e in range(1, B):
                    for db in (1, -1):
                        events.append((when + 0.95 * e, 1, h, "b", d, da, e, db))
                for e in range(B):
                    for db in (1, -1) if e else (0,):
                        events.append((last + 0.75, 2, h, "core", d, da, e, db))
            events.append((last + 0.75, 3, 0, "group", d, da, 0, 0))
    return sorted(events, key=lambda ev: ev[:2])


def body(
    A, B, steps, pw,
    owners, blocks, valence, panel, conduction, out,
    v_all, panel_v, cond_v, t_all, r_all, s_all,
    load_sems, g1_recv, g1_a, g1_b, g1_c, g2_recv, g2_a, g2_b, g2_c, x_send, x_recv,
):
    n = A * B * 2
    rows = valence.shape[0]
    me = lax.axis_index("pair")
    c = lax.rem(me, 2)
    chip = lax.div(me, 2)
    b = lax.rem(chip, B)
    a = lax.div(chip, B)

    def at(aa, bb, cc):
        return (aa * B + bb) * 2 + cc

    load_v = pltpu.make_async_copy(valence, v_all.at[me], load_sems.at[0])
    load_p = pltpu.make_async_copy(panel.at[0], panel_v, load_sems.at[1])
    load_c = [
        pltpu.make_async_copy(conduction.at[:, pl.ds(k * pw, pw)], cond_v.at[k], load_sems.at[2 + k])
        for k in range(cond_v.shape[0])
    ]
    load_v.start()
    load_p.start()
    for load in load_c:
        load.start()

    barrier = pltpu.get_barrier_semaphore()
    near = [
        *((a >= hop, at(a - hop, b, c)) for hop in range(1, REACH + 1)),
        *((a + hop < A, at(a + hop, b, c)) for hop in range(1, REACH + 1)),
        (b > 0, at(a, b - 1, c)),
        (b < B - 1, at(a, b + 1, c)),
    ]
    count = jnp.int32(1)
    for there, who in near:
        count = count + there.astype(jnp.int32)

        @pl.when(there)
        def _():
            pl.semaphore_signal(barrier, inc=1, device_id={"pair": who}, device_id_type=MESH)

    pl.semaphore_signal(barrier, inc=1, device_id={"pair": at(a, b, 1 - c)}, device_id_type=MESH)
    pl.semaphore_wait(barrier, count)

    def gather(view, recv, sem_a, sem_b, sem_c, on_group):
        def copy(idx, h, sem, who):
            return pltpu.make_async_remote_copy(
                src_ref=view(idx, h), dst_ref=view(idx, h), send_sem=sem, recv_sem=recv.at[h, idx],
                device_id={"pair": who}, device_id_type=MESH,
            )

        drains = []

        def send(cond, idx, h, sem, who):
            @pl.when(cond)
            def _():
                copy(idx, h, sem, who).start()

            def drain():
                @pl.when(cond)
                def _():
                    copy(idx, h, sem, who).wait_send()

            drains.append(drain)

        def arrived(idx, h):
            copy(idx, h, sem_c.at[h, 0], me).wait_recv()

        for _, _, h, kind, d, da, e, db in events_of(A, B):
            sa, sb = a - d * da, b - e * db
            there = (sa >= 0) & (sa < A) & (sb >= 0) & (sb < B)
            if kind == "a":
                idx = at(sa, b, c)
                if d:
                    @pl.when(there)
                    def _():
                        arrived(idx, h)
                for hop in range(1, REACH + 1) if d % REACH == 0 else ():
                    if da >= 0:
                        send(there & (a + hop < A), idx, h, sem_a.at[h, hop - 1, sa], at(a + hop, b, c))
                    if da <= 0:
                        send(there & (a >= hop), idx, h, sem_a.at[h, REACH - 1 + hop, sa], at(a - hop, b, c))
                send(there & (b < B - 1), idx, h, sem_b.at[h, 0, sa * B + b], at(a, b + 1, c))
                send(there & (b > 0), idx, h, sem_b.at[h, 1, sa * B + b], at(a, b - 1, c))
                send(there, idx, h, sem_c.at[h, sa * B + b], at(a, b, 1 - c))
            elif kind == "b":
                idx = at(sa, sb, c)

                @pl.when(there)
                def _():
                    arrived(idx, h)

                if db > 0:
                    send(there & (b < B - 1), idx, h, sem_b.at[h, 0, sa * B + sb], at(a, b + 1, c))
                else:
                    send(there & (b > 0), idx, h, sem_b.at[h, 1, sa * B + sb], at(a, b - 1, c))
                send(there, idx, h, sem_c.at[h, sa * B + sb], at(a, b, 1 - c))
            elif kind == "core":
                @pl.when(there)
                def _():
                    arrived(at(sa, sb, 1 - c), h)
            else:
                @pl.when(there)
                def _():
                    on_group(sa)
        return drains

    group = 2 * B
    drains = []

    def exchange(dst):
        return pltpu.make_async_remote_copy(
            src_ref=t_all.at[dst], dst_ref=r_all.at[me], send_sem=x_send.at[dst], recv_sem=x_recv.at[me],
            device_id={"pair": dst}, device_id_type=MESH,
        )

    def contract_group(sa):
        first = sa * group
        left = v_all[pl.ds(first, group)].reshape(group * rows, v_all.shape[2])
        product = jnp.dot(left, panel_v[...], preferred_element_type=jnp.float32)
        t_all[pl.ds(first, group)] = product.reshape(group, rows, pw)
        for k in range(group):
            dst = first + k

            @pl.when(dst != me)
            def _():
                exchange(dst).start()

    half_v = v_all.shape[2] // PIECES
    half_s = s_all.shape[1] // PIECES

    def valence_view(idx, h):
        return v_all.at[idx, :, pl.ds(h * half_v, half_v)]

    def chosen_view(idx, h):
        return s_all.at[idx, pl.ds(h * half_s, half_s)]

    load_v.wait()
    load_p.wait()
    drains += gather(valence_view, g1_recv, g1_a, g1_b, g1_c, contract_group)
    for load in load_c:
        load.wait()

    r_all[me] = t_all[me]
    wanted = [jnp.full((rows, pw), owners[s], jnp.int32) for s in range(steps)]

    def take(k, sums):
        @pl.when(k != me)
        def _():
            pltpu.make_async_remote_copy(
                src_ref=t_all.at[k], dst_ref=r_all.at[k], send_sem=x_send.at[k], recv_sem=x_recv.at[k],
                device_id={"pair": k}, device_id_type=MESH,
            ).wait_recv()
        value = r_all[k]
        return tuple(jnp.where(w == k, value, total) for w, total in zip(wanted, sums))

    chosen = lax.fori_loop(0, n, take, (jnp.zeros((rows, pw), jnp.float32),) * steps)
    for s in range(steps):
        value = chosen[s]
        high = value.astype(jnp.bfloat16)
        s_all[me, 2 * s] = high
        s_all[me, 2 * s + 1] = (value - high.astype(jnp.float32)).astype(jnp.bfloat16)

    def output_group(sa):
        first = sa * group
        height = group * rows
        total = jnp.zeros((2 * height, out.shape[1]), jnp.float32)
        for s in range(steps):
            left = jnp.concatenate(
                [s_all[pl.ds(first, group), 2 * s + h].reshape(height, pw) for h in (0, 1)], axis=0
            )
            right = cond_v[blocks[s]]
            total = total + lax.dot_general(
                left, right, (((1,), (1,)), ((), ())), preferred_element_type=jnp.float32
            )
        result = total[:height] + total[height:]
        out[pl.ds(pl.multiple_of(first * rows, height), height), :] = result.astype(out.dtype)

    drains += gather(chosen_view, g2_recv, g2_a, g2_b, g2_c, output_group)

    def drain_exchange(k, carry):
        @pl.when(k != me)
        def _():
            exchange(k).wait_send()
        return carry

    lax.fori_loop(0, n, drain_exchange, 0)
    for drain in drains:
        drain()


def solution(mesh):
    n = mesh.shape["pair"]
    A, B = grid_of(n)

    def per_device(screened, conduction, valence, owners, column_block):
        steps = owners.shape[0]
        rows, ng = valence.shape
        pw = screened.shape[2]
        cols = conduction.shape[0]
        dma = pltpu.SemaphoreType.DMA
        sems = [dma((PIECES, n)), dma((PIECES, 2 * REACH, A)), dma((PIECES, 2, A * B)), dma((PIECES, A * B))]
        smem = pl.BlockSpec(memory_space=pltpu.SMEM)
        hbm = pl.BlockSpec(memory_space=pl.ANY)
        return pl.pallas_call(
            functools.partial(body, A, B, steps, pw),
            out_shape=jax.ShapeDtypeStruct((n * rows, cols), jnp.bfloat16),
            in_specs=[smem, smem, hbm, hbm, hbm],
            out_specs=pl.BlockSpec(memory_space=pltpu.VMEM),
            scratch_shapes=[
                pltpu.VMEM((n, rows, ng), jnp.bfloat16),
                pltpu.VMEM((ng, pw), jnp.bfloat16),
                pltpu.VMEM((ng // pw, cols, pw), jnp.bfloat16),
                pltpu.VMEM((n, rows, pw), jnp.float32),
                pltpu.VMEM((n, rows, pw), jnp.float32),
                pltpu.VMEM((n, 2 * steps, rows, pw), jnp.bfloat16),
                dma((2 + ng // pw,)),
                *sems,
                *sems,
                dma((n,)),
                dma((n,)),
            ],
            compiler_params=pltpu.CompilerParams(collective_id=0, has_side_effects=True),
            name="bse_direct",
        )(owners, column_block, valence, screened, conduction)

    placed = (
        P(("pb", "pair"), None, None),
        P(("pb", "pair"), None),
        P(("pb", "pair"), None),
        P("pb"),
        P("pb"),
    )
    return jax.shard_map(per_device, mesh=mesh, in_specs=placed, out_specs=P("pb", "pair"), check_vma=False)
```

profile of v0, /device:TPU:0, one launch (start us, length us, event | category | flops | bytes accessed | tf_op | source)
XLA Modules:
  0.0 40.9 jit_solution(268291825044094229)
XLA Ops:
  0.0 39.1 %bse_direct.1 = bf16[256,640]{1,0:T(8,128)(2,1)} custom-call(s32[4]{0:T(128)} %owners.1, s32[4]{0:T(128)} %blocks.1, bf16[16,2048]{1,0:T(8,128)(2,1)} %valence.1, bf16[1,2048,256]{2,1,0:T(8,128)(2,1)} %panel.1, bf16[640,2048]{1,0:T(8,128)(2,1)} %conduction.1), custom_call_target="tpu_custom_call" | custom-call | tf_op jit(solution)/shard_map/bse_direct/pallas_call | solution.py:248
  39.1 1.7 %copy.7 = bf16[256,640]{1,0:T(8,128)(2,1)} copy(bf16[256,640]{1,0:T(8,128)(2,1)} %bse_direct.1) | data formatting | bytes 655360
where the time goes:
time: 41 us; the launch traced here: 40.9 us
  Pallas kernels  39.1 us (95%)
  local copies, waits for them, and re-layouts  1.73 us (4%)
    pallas_call x1, Pallas kernels, per_device(): pl.pallas_call(functools.partial(body, A, B, steps, pw), out_shape=jax.Sh...  39.1 us
    unnamed x1, local copies, waits for them, and re-layouts  1.73 us

commit v1 on v0

v1 whole, which is shorter than its diff:
```python
import functools

import jax
import jax.numpy as jnp
from jax import lax
from jax.experimental import pallas as pl
from jax.experimental.pallas import tpu as pltpu
from jax.sharding import PartitionSpec as P

MESH = pl.DeviceIdType.MESH
REACH = 3
PIECES = 1
LANES = 128
TOP = 32000.0
LOG2E = 1.4426950408889634
SPACE = pl.ANY


def grid_of(n):
    chips = n // 2
    b = 1
    while b * b * 4 <= chips:
        b *= 2
    return chips // b, b


def events_of(A, B):
    events = []
    for d in range(A):
        start = 1.0 * (-(-d // REACH)) + 0.3 * ((d - 1) % REACH if d else 0)
        last = start + 0.95 * (B - 1)
        for da in (1, -1) if d else (0,):
            for h in range(PIECES):
                when = start + 0.3 * h / PIECES
                events.append((when, 0, h, "a", d, da, 0, 0))
                for e in range(1, B):
                    for db in (1, -1):
                        events.append((when + 0.95 * e, 1, h, "b", d, da, e, db))
                for e in range(B):
                    for db in (1, -1) if e else (0,):
                        events.append((last + 0.75, 2, h, "core", d, da, e, db))
            events.append((last + 0.75, 3, 0, "group", d, da, 0, 0))
    return sorted(events, key=lambda ev: ev[:2])


def body(
    A, B, steps, pw,
    owners, blocks, valence, panel, conduction, out,
    v_all, pan, cond_v, cond_s, t_all, r_all, s_all,
    load_sems, p_send, p_recv, g1_recv, g1_a, g1_b, g1_c, g2_recv, g2_a, g2_b, g2_c, x_send, x_recv,
):
    n = A * B * 2
    chips = A * B
    rows, ng = valence.shape
    tiles = pw // LANES
    parcel = 2 * tiles + 1
    width = LANES // steps
    me = lax.axis_index("pair")
    c = lax.rem(me, 2)
    chip = lax.div(me, 2)
    b = lax.rem(chip, B)
    a = lax.div(chip, B)

    def at(aa, bb, cc):
        return (aa * B + bb) * 2 + cc

    def chip_of(idx):
        return lax.div(idx, 2)

    load_v = pltpu.make_async_copy(valence, v_all.at[chip], load_sems.at[0])
    load_p = pltpu.make_async_copy(panel.at[0], pan.at[c], load_sems.at[1])
    load_c = [
        pltpu.make_async_copy(conduction.at[:, pl.ds(k * pw, pw)], cond_v.at[k], load_sems.at[2 + k])
        for k in range(cond_v.shape[0])
    ]
    load_v.start()
    load_p.start()
    for load in load_c:
        load.start()

    barrier = pltpu.get_barrier_semaphore()
    near = [
        *((a >= hop, at(a - hop, b, c)) for hop in range(1, REACH + 1)),
        *((a + hop < A, at(a + hop, b, c)) for hop in range(1, REACH + 1)),
        (b > 0, at(a, b - 1, c)),
        (b < B - 1, at(a, b + 1, c)),
    ]
    count = jnp.int32(1)
    for there, who in near:
        count = count + there.astype(jnp.int32)

        @pl.when(there)
        def _():
            pl.semaphore_signal(barrier, inc=1, device_id={"pair": who}, device_id_type=MESH)

    twin = at(a, b, 1 - c)
    pl.semaphore_signal(barrier, inc=1, device_id={"pair": twin}, device_id_type=MESH)
    pl.semaphore_wait(barrier, count)

    def gather(view, recv, sem_a, sem_b, sem_c, on_group, cross, idle):
        def copy(idx, h, sem, who):
            return pltpu.make_async_remote_copy(
                src_ref=view(idx, h), dst_ref=view(idx, h), send_sem=sem, recv_sem=recv.at[h, idx],
                device_id={"pair": who}, device_id_type=MESH,
            )

        drains = []

        def send(cond, idx, h, sem, who):
            @pl.when(cond)
            def _():
                copy(idx, h, sem, who).start()

            def drain():
                @pl.when(cond)
                def _():
                    copy(idx, h, sem, who).wait_send()

            drains.append(drain)

        def arrived(idx, h):
            copy(idx, h, sem_a.at[h, 0, 0], me).wait_recv()

        first = True
        for _, _, h, kind, d, da, e, db in events_of(A, B):
            sa, sb = a - d * da, b - e * db
            there = (sa >= 0) & (sa < A) & (sb >= 0) & (sb < B)
            if kind == "a":
                idx = at(sa, b, c)
                if d:
                    @pl.when(there)
                    def _():
                        arrived(idx, h)
                for hop in range(1, REACH + 1) if d % REACH == 0 else ():
                    if da >= 0:
                        send(there & (a + hop < A), idx, h, sem_a.at[h, hop - 1, sa], at(a + hop, b, c))
                    if da <= 0:
                        send(there & (a >= hop), idx, h, sem_a.at[h, REACH - 1 + hop, sa], at(a - hop, b, c))
                send(there & (b < B - 1), idx, h, sem_b.at[h, 0, sa * B + b], at(a, b + 1, c))
                send(there & (b > 0), idx, h, sem_b.at[h, 1, sa * B + b], at(a, b - 1, c))
                if cross:
                    send(there, idx, h, sem_c.at[h, sa * B + b], twin)
            elif kind == "b":
                if first:
                    idle()
                    first = False
                idx = at(sa, sb, c)

                @pl.when(there)
                def _():
                    arrived(idx, h)

                if db > 0:
                    send(there & (b < B - 1), idx, h, sem_b.at[h, 0, sa * B + sb], at(a, b + 1, c))
                else:
                    send(there & (b > 0), idx, h, sem_b.at[h, 1, sa * B + sb], at(a, b - 1, c))
                if cross:
                    send(there, idx, h, sem_c.at[h, sa * B + sb], twin)
            elif kind == "core":
                if cross:
                    @pl.when(there)
                    def _():
                        arrived(at(sa, sb, 1 - c), h)
            else:
                @pl.when(there)
                def _():
                    on_group(sa)
        return drains

    group = 2 * B
    drains = []

    def exchange(dst):
        return pltpu.make_async_remote_copy(
            src_ref=t_all.at[pl.ds(dst * parcel, parcel)], dst_ref=r_all.at[pl.ds(chip * parcel, parcel)],
            send_sem=x_send.at[dst], recv_sem=x_recv.at[chip],
            device_id={"pair": dst * 2 + c}, device_id_type=MESH,
        )

    def contract_group(sa):
        first = sa * B
        height = B * rows
        left = v_all[pl.ds(first, B)].reshape(height, ng)
        lane = lax.broadcasted_iota(jnp.int32, (height, LANES), 1)
        levels = []
        for p in range(2):
            product = jnp.dot(left, pan[p], preferred_element_type=jnp.float32)
            top = jnp.maximum(jnp.max(jnp.abs(product), axis=1, keepdims=True), 1e-33)
            level = jnp.ceil(jnp.log(top) * LOG2E + 1e-3)
            scaled = product * (jnp.exp2(-level) * TOP)
            whole = (scaled + jnp.where(scaled >= 0, 0.5, -0.5)).astype(jnp.int32)
            for j in range(tiles):
                part = whole[:, j * LANES:(j + 1) * LANES].astype(jnp.int16)
                for k in range(B):
                    t_all[(first + k) * parcel + p * tiles + j] = part[k * rows:(k + 1) * rows]
            levels.append(jnp.broadcast_to(level.astype(jnp.int32), (height, LANES)))
        mark = jnp.where(lane < LANES // 2, levels[0], levels[1]).astype(jnp.int16)
        for k in range(B):
            t_all[(first + k) * parcel + 2 * tiles] = mark[k * rows:(k + 1) * rows]
        for k in range(B):
            dst = first + k

            @pl.when(dst != chip)
            def _():
                exchange(dst).start()

    def twin_panel():
        return pltpu.make_async_remote_copy(
            src_ref=pan.at[c], dst_ref=pan.at[c], send_sem=p_send.at[0], recv_sem=p_recv.at[0],
            device_id={"pair": twin}, device_id_type=MESH,
        )

    half_v = ng // PIECES

    def valence_view(idx, h):
        return v_all.at[chip_of(idx), :, pl.ds(h * half_v, half_v)]

    def chosen_view(idx, h):
        return s_all.at[idx]

    def settle():
        load_p.wait()
        twin_panel().start()
        for load in load_c:
            load.wait()
        for s in range(steps):
            cond_s[:, s * pw:(s + 1) * pw] = cond_v[blocks[s]]
        twin_panel().wait()

    load_v.wait()
    drains += gather(valence_view, g1_recv, g1_a, g1_b, g1_c, contract_group, False, settle)

    for k in range(parcel):
        r_all[chip * parcel + k] = t_all[chip * parcel + k]

    def take(k, carry):
        @pl.when(k != chip)
        def _():
            pltpu.make_async_remote_copy(
                src_ref=t_all.at[pl.ds(k * parcel, parcel)], dst_ref=r_all.at[pl.ds(k * parcel, parcel)],
                send_sem=x_send.at[k], recv_sem=x_recv.at[k],
                device_id={"pair": k * 2 + c}, device_id_type=MESH,
            ).wait_recv()
        return carry

    lax.fori_loop(0, chips, take, 0)
    lane = lax.broadcasted_iota(jnp.int32, (rows, LANES), 1)
    marks = jnp.zeros((rows, LANES), jnp.int32)
    for s in range(steps):
        who = owners[s]
        base = lax.div(who, 2) * parcel
        side = lax.rem(who, 2)
        for j in range(tiles):
            s_all[me, s * tiles + j] = r_all[base + side * tiles + j]
        both = r_all[base + 2 * tiles].astype(jnp.int32)
        odd = jnp.full((rows, LANES), side, jnp.int32) == 1
        level = jnp.where(
            odd,
            jnp.broadcast_to(both[:, LANES // 2:LANES // 2 + 1], (rows, LANES)),
            jnp.broadcast_to(both[:, 0:1], (rows, LANES)),
        )
        marks = jnp.where(lax.div(lane, width) == s, level, marks)
    s_all[me, steps * tiles] = marks.astype(jnp.int16)

    def output_group(sa):
        first = sa * group
        height = group * rows
        marks = s_all[pl.ds(first, group), steps * tiles].reshape(height, LANES)
        scale = jnp.exp2(marks.astype(jnp.int32).astype(jnp.float32)) * (1.0 / TOP)
        highs, lows = [], []
        for s in range(steps):
            factor = jnp.broadcast_to(scale[:, s * width:s * width + 1], (height, LANES))
            for j in range(tiles):
                value = s_all[pl.ds(first, group), s * tiles + j].reshape(height, LANES)
                value = value.astype(jnp.int32).astype(jnp.float32) * factor
                high = value.astype(jnp.bfloat16)
                highs.append(high)
                lows.append((value - high.astype(jnp.float32)).astype(jnp.bfloat16))
        left = jnp.concatenate([jnp.concatenate(highs, axis=1), jnp.concatenate(lows, axis=1)], axis=0)
        total = lax.dot_general(
            left, cond_s[...], (((1,), (1,)), ((), ())), preferred_element_type=jnp.float32
        )
        result = total[:height] + total[height:]
        out[pl.ds(pl.multiple_of(first * rows, height), height), :] = result.astype(out.dtype)

    drains += gather(chosen_view, g2_recv, g2_a, g2_b, g2_c, output_group, True, lambda: None)

    def drain_exchange(k, carry):
        @pl.when(k != chip)
        def _():
            exchange(k).wait_send()
        return carry

    lax.fori_loop(0, chips, drain_exchange, 0)
    for drain in drains:
        drain()


def solution(mesh):
    n = mesh.shape["pair"]
    A, B = grid_of(n)

    def per_device(screened, conduction, valence, owners, column_block):
        steps = owners.shape[0]
        rows, ng = valence.shape
        pw = screened.shape[2]
        cols = conduction.shape[0]
        chips = A * B
        parcel = 2 * (pw // LANES) + 1
        dma = pltpu.SemaphoreType.DMA
        sems = [dma((PIECES, n)), dma((PIECES, 2 * REACH, A)), dma((PIECES, 2, chips)), dma((PIECES, chips))]
        smem = pl.BlockSpec(memory_space=pltpu.SMEM)
        hbm = pl.BlockSpec(memory_space=SPACE)
        return pl.pallas_call(
            functools.partial(body, A, B, steps, pw),
            out_shape=jax.ShapeDtypeStruct((n * rows, cols), jnp.bfloat16),
            in_specs=[smem, smem, hbm, hbm, hbm],
            out_specs=pl.BlockSpec(memory_space=pltpu.VMEM),
            scratch_shapes=[
                pltpu.VMEM((chips, rows, ng), jnp.bfloat16),
                pltpu.VMEM((2, ng, pw), jnp.bfloat16),
                pltpu.VMEM((ng // pw, cols, pw), jnp.bfloat16),
                pltpu.VMEM((cols, steps * pw), jnp.bfloat16),
                pltpu.VMEM((chips * parcel, rows, LANES), jnp.int16),
                pltpu.VMEM((chips * parcel, rows, LANES), jnp.int16),
                pltpu.VMEM((n, steps * (pw // LANES) + 1, rows, LANES), jnp.int16),
                dma((2 + ng // pw,)),
                dma((1,)),
                dma((1,)),
                *sems,
                *sems,
                dma((chips,)),
                dma((chips,)),
            ],
            compiler_params=pltpu.CompilerParams(collective_id=0, has_side_effects=True),
            name="bse_direct",
        )(owners, column_block, valence, screened, conduction)

    placed = (
        P(("pb", "pair"), None, None),
        P(("pb", "pair"), None),
        P(("pb", "pair"), None),
        P("pb"),
        P("pb"),
    )
    return jax.shard_map(per_device, mesh=mesh, in_specs=placed, out_specs=P("pb", "pair"), check_vma=False)
```

time: 41 us -> 37.7 us (0.920)
  Pallas kernels: 39.1 us -> 35.8 us
    pallas_call x1, Pallas kernels: 39.1 us -> 35.8 us  [per_device(): pl.pallas_call(functools.partial(body, A, B, steps, pw), out_shape=jax.Sh...]
where the time goes in v1:
time: 37.7 us; the launch traced here: 37.6 us
  Pallas kernels  35.8 us (95%)
  local copies, waits for them, and re-layouts  1.73 us (5%)
    pallas_call x1, Pallas kernels, per_device(): pl.pallas_call(functools.partial(body, A, B, steps, pw), out_shape=jax.Sh...  35.8 us
    unnamed x1, local copies, waits for them, and re-layouts  1.73 us

profile of v1, /device:TPU:0, one launch (start us, length us, event | category | flops | bytes accessed | tf_op | source)
XLA Modules:
  0.0 37.6 jit_solution(6897931045176693759)
XLA Ops:
  0.0 35.8 %bse_direct.1 = bf16[256,640]{1,0:T(8,128)(2,1)} custom-call(s32[4]{0:T(128)} %owners.1, s32[4]{0:T(128)} %blocks.1, bf16[16,2048]{1,0:T(8,128)(2,1)} %valence.1, bf16[1,2048,256]{2,1,0:T(8,128)(2,1)} %panel.1, bf16[640,2048]{1,0:T(8,128)(2,1)} %conduction.1), custom_call_target="tpu_custom_call" | custom-call | tf_op jit(solution)/shard_map/bse_direct/pallas_call | solution.py:314
  35.8 1.7 %copy.7 = bf16[256,640]{1,0:T(8,128)(2,1)} copy(bf16[256,640]{1,0:T(8,128)(2,1)} %bse_direct.1) | data formatting | bytes 655360

commit v2 on v1

--- a/solution.py
+++ b/solution.py
@@ -10,6 +10,8 @@
 MESH = pl.DeviceIdType.MESH
 REACH = 3
 PIECES = 1
+LATE = 0.0
+DIRECT = (1, 3)
 LANES = 128
 TOP = 32000.0
 LOG2E = 1.4426950408889634
@@ -24,11 +26,12 @@
     return chips // b, b
 
 
-def events_of(A, B):
+def events_of(A, B, cross):
     events = []
     for d in range(A):
         start = 1.0 * (-(-d // REACH)) + 0.3 * ((d - 1) % REACH if d else 0)
         last = start + 0.95 * (B - 1)
+        settled = last + (0.75 if cross else 0.0)
         for da in (1, -1) if d else (0,):
             for h in range(PIECES):
                 when = start + 0.3 * h / PIECES
@@ -36,10 +39,11 @@
                 for e in range(1, B):
                     for db in (1, -1):
                         events.append((when + 0.95 * e, 1, h, "b", d, da, e, db))
-                for e in range(B):
-                    for db in (1, -1) if e else (0,):
-                        events.append((last + 0.75, 2, h, "core", d, da, e, db))
-            events.append((last + 0.75, 3, 0, "group", d, da, 0, 0))
+                if cross:
+                    for e in range(B):
+                        for db in (1, -1) if e else (0,):
+                            events.append((settled, 2, h, "core", d, da, e, db))
+            events.append((settled + LATE, 3, 0, "group", d, da, 0, 0))
     return sorted(events, key=lambda ev: ev[:2])
 
 
@@ -47,7 +51,7 @@
     A, B, steps, pw,
     owners, blocks, valence, panel, conduction, out,
     v_all, pan, cond_v, cond_s, t_all, r_all, s_all,
-    load_sems, p_send, p_recv, g1_recv, g1_a, g1_b, g1_c, g2_recv, g2_a, g2_b, g2_c, x_send, x_recv,
+    load_sems, up, down, p_send, p_recv, g1_recv, g1_a, g1_b, g1_c, g1_d, g2_recv, g2_a, g2_b, g2_c, g2_d, x_send, x_recv,
 ):
     n = A * B * 2
     chips = A * B
@@ -80,8 +84,8 @@
 
     barrier = pltpu.get_barrier_semaphore()
     near = [
-        *((a >= hop, at(a - hop, b, c)) for hop in range(1, REACH + 1)),
-        *((a + hop < A, at(a + hop, b, c)) for hop in range(1, REACH + 1)),
+        (a > 0, at(a - 1, b, c)),
+        (a < A - 1, at(a + 1, b, c)),
         (b > 0, at(a, b - 1, c)),
         (b < B - 1, at(a, b + 1, c)),
     ]
@@ -97,7 +101,25 @@
     pl.semaphore_signal(barrier, inc=1, device_id={"pair": twin}, device_id_type=MESH)
     pl.semaphore_wait(barrier, count)
 
-    def gather(view, recv, sem_a, sem_b, sem_c, on_group, cross, idle):
+    def tell(hop):
+        @pl.when((a > 0) & (a + hop - 1 < A))
+        def _():
+            pl.semaphore_signal(up.at[hop - 2], inc=1, device_id={"pair": at(a - 1, b, c)}, device_id_type=MESH)
+
+        @pl.when((a < A - 1) & (a >= hop - 1))
+        def _():
+            pl.semaphore_signal(down.at[hop - 2], inc=1, device_id={"pair": at(a + 1, b, c)}, device_id_type=MESH)
+
+    def hear(hop):
+        @pl.when(a + hop < A)
+        def _():
+            pl.semaphore_wait(up.at[hop - 2], 1)
+
+        @pl.when(a >= hop)
+        def _():
+            pl.semaphore_wait(down.at[hop - 2], 1)
+
+    def gather(view, recv, sem_a, sem_b, sem_c, sem_d, on_group, cross, direct, staged):
         def copy(idx, h, sem, who):
             return pltpu.make_async_remote_copy(
                 src_ref=view(idx, h), dst_ref=view(idx, h), send_sem=sem, recv_sem=recv.at[h, idx],
@@ -121,8 +143,7 @@
         def arrived(idx, h):
             copy(idx, h, sem_a.at[h, 0, 0], me).wait_recv()
 
-        first = True
-        for _, _, h, kind, d, da, e, db in events_of(A, B):
+        for _, _, h, kind, d, da, e, db in events_of(A, B, cross):
             sa, sb = a - d * da, b - e * db
             there = (sa >= 0) & (sa < A) & (sb >= 0) & (sb < B)
             if kind == "a":
@@ -131,19 +152,28 @@
                     @pl.when(there)
                     def _():
                         arrived(idx, h)
-                for hop in range(1, REACH + 1) if d % REACH == 0 else ():
+                if d not in direct:
+                    send(there & (b < B - 1), idx, h, sem_b.at[h, 0, sa * B + b], at(a, b + 1, c))
+                    send(there & (b > 0), idx, h, sem_b.at[h, 1, sa * B + b], at(a, b - 1, c))
+                first = staged is not None and d == 0 and h == 0
+                order = range(1, REACH + 1)
+                for hop in order if d % REACH == 0 else ():
+                    if first and hop > 1:
+                        staged(hop)
                     if da >= 0:
                         send(there & (a + hop < A), idx, h, sem_a.at[h, hop - 1, sa], at(a + hop, b, c))
                     if da <= 0:
                         send(there & (a >= hop), idx, h, sem_a.at[h, REACH - 1 + hop, sa], at(a - hop, b, c))
-                send(there & (b < B - 1), idx, h, sem_b.at[h, 0, sa * B + b], at(a, b + 1, c))
-                send(there & (b > 0), idx, h, sem_b.at[h, 1, sa * B + b], at(a, b - 1, c))
+                    if d == 0 and hop in direct:
+                        for way, db in enumerate((1, -1)):
+                            beside = (b + db >= 0) & (b + db < B)
+                            send(beside & (a + hop < A), idx, h, sem_d.at[h, way, hop - 1], at(a + hop, b + db, c))
+                            send(beside & (a >= hop), idx, h, sem_d.at[h, way, REACH - 1 + hop], at(a - hop, b + db, c))
+                if first:
+                    staged(0)
                 if cross:
                     send(there, idx, h, sem_c.at[h, sa * B + b], twin)
             elif kind == "b":
-                if first:
-                    idle()
-                    first = False
                 idx = at(sa, sb, c)
 
                 @pl.when(there)
@@ -162,6 +192,9 @@
                     def _():
                         arrived(at(sa, sb, 1 - c), h)
             else:
+                if d == 0 and not cross:
+                    twin_panel().wait_recv()
+
                 @pl.when(there)
                 def _():
                     on_group(sa)
@@ -218,17 +251,22 @@
     def chosen_view(idx, h):
         return s_all.at[idx]
 
-    def settle():
-        load_p.wait()
-        twin_panel().start()
-        for load in load_c:
-            load.wait()
-        for s in range(steps):
-            cond_s[:, s * pw:(s + 1) * pw] = cond_v[blocks[s]]
-        twin_panel().wait()
-
+    def staged(hop):
+        if hop:
+            hear(hop)
+            if hop < REACH:
+                tell(hop + 1)
+        else:
+            for load in load_c:
+                load.wait()
+            for s in range(steps):
+                cond_s[:, s * pw:(s + 1) * pw] = cond_v[blocks[s]]
+
+    tell(2)
     load_v.wait()
-    drains += gather(valence_view, g1_recv, g1_a, g1_b, g1_c, contract_group, False, settle)
+    load_p.wait()
+    twin_panel().start()
+    drains += gather(valence_view, g1_recv, g1_a, g1_b, g1_c, g1_d, contract_group, False, (), staged)
 
     for k in range(parcel):
         r_all[chip * parcel + k] = t_all[chip * parcel + k]
@@ -283,7 +321,7 @@
         result = total[:height] + total[height:]
         out[pl.ds(pl.multiple_of(first * rows, height), height), :] = result.astype(out.dtype)
 
-    drains += gather(chosen_view, g2_recv, g2_a, g2_b, g2_c, output_group, True, lambda: None)
+    drains += gather(chosen_view, g2_recv, g2_a, g2_b, g2_c, g2_d, output_group, True, DIRECT, None)
 
     def drain_exchange(k, carry):
         @pl.when(k != chip)
@@ -291,6 +329,7 @@
             exchange(k).wait_send()
         return carry
 
+    twin_panel().wait_send()
     lax.fori_loop(0, chips, drain_exchange, 0)
     for drain in drains:
         drain()
@@ -308,7 +347,7 @@
         chips = A * B
         parcel = 2 * (pw // LANES) + 1
         dma = pltpu.SemaphoreType.DMA
-        sems = [dma((PIECES, n)), dma((PIECES, 2 * REACH, A)), dma((PIECES, 2, chips)), dma((PIECES, chips))]
+        sems = [dma((PIECES, n)), dma((PIECES, 2 * REACH, A)), dma((PIECES, 2, chips)), dma((PIECES, chips)), dma((PIECES, 2, 2 * REACH))]
         smem = pl.BlockSpec(memory_space=pltpu.SMEM)
         hbm = pl.BlockSpec(memory_space=SPACE)
         return pl.pallas_call(
@@ -325,6 +364,8 @@
                 pltpu.VMEM((chips * parcel, rows, LANES), jnp.int16),
                 pltpu.VMEM((n, steps * (pw // LANES) + 1, rows, LANES), jnp.int16),
                 dma((2 + ng // pw,)),
+                pltpu.SemaphoreType.REGULAR((REACH - 1,)),
+                pltpu.SemaphoreType.REGULAR((REACH - 1,)),
                 dma((1,)),
                 dma((1,)),
                 *sems,

time: 37.7 us -> 35.7 us (0.947)
  Pallas kernels: 35.8 us -> 33.8 us
    pallas_call x1, Pallas kernels: 35.8 us -> 33.8 us  [per_device(): pl.pallas_call(functools.partial(body, A, B, steps, pw), out_shape=jax.Sh...]
where the time goes in v2:
time: 35.7 us; the launch traced here: 35.6 us
  Pallas kernels  33.8 us (95%)
  local copies, waits for them, and re-layouts  1.73 us (5%)
    pallas_call x1, Pallas kernels, per_device(): pl.pallas_call(functools.partial(body, A, B, steps, pw), out_shape=jax.Sh...  33.8 us
    unnamed x1, local copies, waits for them, and re-layouts  1.73 us

profile of v2, /device:TPU:0, one launch (start us, length us, event | category | flops | bytes accessed | tf_op | source)
XLA Modules:
  0.0 35.6 jit_solution(10228095401718396138)
XLA Ops:
  0.0 33.8 %bse_direct.1 = bf16[256,640]{1,0:T(8,128)(2,1)} custom-call(s32[4]{0:T(128)} %owners.1, s32[4]{0:T(128)} %blocks.1, bf16[16,2048]{1,0:T(8,128)(2,1)} %valence.1, bf16[1,2048,256]{2,1,0:T(8,128)(2,1)} %panel.1, bf16[640,2048]{1,0:T(8,128)(2,1)} %conduction.1), custom_call_target="tpu_custom_call" | custom-call | tf_op jit(solution)/shard_map/bse_direct/pallas_call | solution.py:353
  33.8 1.7 %copy.7 = bf16[256,640]{1,0:T(8,128)(2,1)} copy(bf16[256,640]{1,0:T(8,128)(2,1)} %bse_direct.1) | data formatting | bytes 655360

commit v3 on v2

--- a/solution.py
+++ b/solution.py
@@ -10,7 +10,7 @@
 MESH = pl.DeviceIdType.MESH
 REACH = 3
 PIECES = 1
-LATE = 0.0
+LATE = 0.1
 DIRECT = (1, 3)
 LANES = 128
 TOP = 32000.0
@@ -26,11 +26,12 @@
     return chips // b, b
 
 
-def events_of(A, B, cross):
+def events_of(A, B, cross, direct):
     events = []
     for d in range(A):
         start = 1.0 * (-(-d // REACH)) + 0.3 * ((d - 1) % REACH if d else 0)
-        last = start + 0.95 * (B - 1)
+        cast = 0.3 * REACH - 0.2 + 0.01 * d if d in direct else start
+        last = cast + 0.95 * (B - 1)
         settled = last + (0.75 if cross else 0.0)
         for da in (1, -1) if d else (0,):
             for h in range(PIECES):
@@ -38,12 +39,12 @@
                 events.append((when, 0, h, "a", d, da, 0, 0))
                 for e in range(1, B):
                     for db in (1, -1):
-                        events.append((when + 0.95 * e, 1, h, "b", d, da, e, db))
+                        events.append((cast + 0.3 * h / PIECES + 0.95 * e, 1, h, "b", d, da, e, db))
                 if cross:
                     for e in range(B):
                         for db in (1, -1) if e else (0,):
                             events.append((settled, 2, h, "core", d, da, e, db))
-            events.append((settled + LATE, 3, 0, "group", d, da, 0, 0))
+            events.append((settled + (0.0 if d or cross else LATE), 3, 0, "group", d, da, 0, 0))
     return sorted(events, key=lambda ev: ev[:2])
 
 
@@ -79,8 +80,6 @@
     ]
     load_v.start()
     load_p.start()
-    for load in load_c:
-        load.start()
 
     barrier = pltpu.get_barrier_semaphore()
     near = [
@@ -100,6 +99,8 @@
     twin = at(a, b, 1 - c)
     pl.semaphore_signal(barrier, inc=1, device_id={"pair": twin}, device_id_type=MESH)
     pl.semaphore_wait(barrier, count)
+    for load in load_c:
+        load.start()
 
     def tell(hop):
         @pl.when((a > 0) & (a + hop - 1 < A))
@@ -143,7 +144,7 @@
         def arrived(idx, h):
             copy(idx, h, sem_a.at[h, 0, 0], me).wait_recv()
 
-        for _, _, h, kind, d, da, e, db in events_of(A, B, cross):
+        for _, _, h, kind, d, da, e, db in events_of(A, B, cross, direct):
             sa, sb = a - d * da, b - e * db
             there = (sa >= 0) & (sa < A) & (sb >= 0) & (sb < B)
             if kind == "a":
@@ -253,6 +254,9 @@
 
     def staged(hop):
         if hop:
+            if hop == 2:
+                load_p.wait()
+                twin_panel().start()
             hear(hop)
             if hop < REACH:
                 tell(hop + 1)
@@ -260,12 +264,10 @@
             for load in load_c:
                 load.wait()
             for s in range(steps):
-                cond_s[:, s * pw:(s + 1) * pw] = cond_v[blocks[s]]
+                cond_s[s * pw:(s + 1) * pw, :] = cond_v[blocks[s]].T
 
     tell(2)
     load_v.wait()
-    load_p.wait()
-    twin_panel().start()
     drains += gather(valence_view, g1_recv, g1_a, g1_b, g1_c, g1_d, contract_group, False, (), staged)
 
     for k in range(parcel):
@@ -316,7 +318,7 @@
                 lows.append((value - high.astype(jnp.float32)).astype(jnp.bfloat16))
         left = jnp.concatenate([jnp.concatenate(highs, axis=1), jnp.concatenate(lows, axis=1)], axis=0)
         total = lax.dot_general(
-            left, cond_s[...], (((1,), (1,)), ((), ())), preferred_element_type=jnp.float32
+            left, cond_s[...], (((1,), (0,)), ((), ())), preferred_element_type=jnp.float32
         )
         result = total[:height] + total[height:]
         out[pl.ds(pl.multiple_of(first * rows, height), height), :] = result.astype(out.dtype)
@@ -359,7 +361,7 @@
                 pltpu.VMEM((chips, rows, ng), jnp.bfloat16),
                 pltpu.VMEM((2, ng, pw), jnp.bfloat16),
                 pltpu.VMEM((ng // pw, cols, pw), jnp.bfloat16),
-                pltpu.VMEM((cols, steps * pw), jnp.bfloat16),
+                pltpu.VMEM((steps * pw, cols), jnp.bfloat16),
                 pltpu.VMEM((chips * parcel, rows, LANES), jnp.int16),
                 pltpu.VMEM((chips * parcel, rows, LANES), jnp.int16),
                 pltpu.VMEM((n, steps * (pw // LANES) + 1, rows, LANES), jnp.int16),

time: 35.7 us -> 34.8 us (0.975)
  Pallas kernels: 33.8 us -> 32.9 us
    pallas_call x1, Pallas kernels: 33.8 us -> 32.9 us  [per_device(): pl.pallas_call(functools.partial(body, A, B, steps, pw), out_shape=jax.Sh...]
where the time goes in v3:
time: 34.8 us; the launch traced here: 34.6 us
  Pallas kernels  32.9 us (95%)
  local copies, waits for them, and re-layouts  1.73 us (5%)
    pallas_call x1, Pallas kernels, per_device(): pl.pallas_call(functools.partial(body, A, B, steps, pw), out_shape=jax.Sh...  32.9 us
    unnamed x1, local copies, waits for them, and re-layouts  1.73 us

profile of v3, /device:TPU:0, one launch (start us, length us, event | category | flops | bytes accessed | tf_op | source)
XLA Modules:
  0.0 34.6 jit_solution(5051937324259013909)
XLA Ops:
  0.0 32.9 %bse_direct.1 = bf16[256,640]{1,0:T(8,128)(2,1)} custom-call(s32[4]{0:T(128)} %owners.1, s32[4]{0:T(128)} %blocks.1, bf16[16,2048]{1,0:T(8,128)(2,1)} %valence.1, bf16[1,2048,256]{2,1,0:T(8,128)(2,1)} %panel.1, bf16[640,2048]{1,0:T(8,128)(2,1)} %conduction.1), custom_call_target="tpu_custom_call" | custom-call | tf_op jit(solution)/shard_map/bse_direct/pallas_call | solution.py:355
  32.9 1.7 %copy.7 = bf16[256,640]{1,0:T(8,128)(2,1)} copy(bf16[256,640]{1,0:T(8,128)(2,1)} %bse_direct.1) | data formatting | bytes 655360
